TPU v7x, 32 devices: a whole 2x2x4 slice. The times are simulated.
32 devices in a mesh: dp: 4 (over x, core), mp: 8 (over z, y).
Axes of the slice: x: 2, y: 2, z: 4, core: 2. Of those that a mesh axis runs over, the one named last changes fastest.
Arguments:
- source_prompts: bfloat16 [128, 64, 4096], P(None, None, 'mp'), may hold values from -6 to 6
- task_logits: float32 [8, 128], replicated, may hold values from -8 to 260
- task_ids: int32 [32], P('dp'), may hold values from 0 to 7
- key_weight: bfloat16 [4096, 4096], P(None, 'mp'), may hold values from -0.09375 to 0.09375
- value_weight: bfloat16 [4096, 4096], P(None, 'mp'), may hold values from -0.09375 to 0.09375
- queries: bfloat16 [32, 128, 4096], P(('dp', 'mp')), may hold values from -32 to 32
- keys: bfloat16 [32, 128, 4096], P(('dp', 'mp')), may hold values from -16 to 16
- values: bfloat16 [32, 128, 4096], P(('dp', 'mp')), may hold values from -6 to 6
- cotangent: bfloat16 [32, 128, 4096], P(('dp', 'mp')), may hold values from -6 to 6
Outputs:
- attended: bfloat16 [32, 128, 4096], P(('dp', 'mp'))
- source_grad: float32 [128, 64, 4096], P(None, 'dp', 'mp')
- logits_grad: float32 [8, 128], replicated
All inputs are finite; a program needn't handle non-finite values.
Results may differ from a plain program's by a relative error of at most 0.011.
Values may be sent and summed in bfloat16 or wider, within the bound.
A program may use at most 128 MiB of HBM per device.

v0:
```python
import jax
import jax.numpy as jnp
from jax import lax
from jax.sharding import PartitionSpec as P

D = 4096
HEADS = 32
DH = 128
NSRC = 128
NTASK = 8
PTOK = 64
SEQ = 128
E_DEV = 1


mask_fill = -1e30


def example_block(prompt_pair, queries, keys, values, cotangent):
    examples = queries.shape[0]
    score_scale = DH ** (-0.5)
    key_all = jnp.concatenate([prompt_pair[:, :, 0, :], keys], axis=1)
    value_all = jnp.concatenate([prompt_pair[:, :, 1, :], values], axis=1)
    query_heads = queries.reshape(examples, SEQ, HEADS, DH)
    key_heads = key_all.reshape(examples, PTOK + SEQ, HEADS, DH)
    value_heads = value_all.reshape(examples, PTOK + SEQ, HEADS, DH)
    cot_heads = cotangent.reshape(examples, SEQ, HEADS, DH)
    scores = (
        jnp.einsum("eihd,ejhd->ehij", query_heads, key_heads, preferred_element_type=jnp.float32)
        * score_scale
    )
    column = jnp.arange(PTOK + SEQ)[None, :]
    position = jnp.arange(SEQ)[:, None]
    visible = (column < PTOK) | (column - PTOK <= position)
    scores = jnp.where(visible[None, None], scores, mask_fill)
    top_score = jnp.max(scores, axis=3, keepdims=True)
    exponent = jnp.exp(scores - top_score)
    attention = exponent / jnp.sum(exponent, axis=3, keepdims=True)
    attention_rounded = attention.astype(jnp.bfloat16)
    attended = jnp.einsum(
        "ehij,ejhd->eihd", attention_rounded, value_heads, preferred_element_type=jnp.float32
    )
    attended = attended.astype(jnp.bfloat16).reshape(examples, SEQ, D)
    grad_attention = jnp.einsum(
        "eihd,ejhd->ehij", cot_heads, value_heads, preferred_element_type=jnp.float32
    )
    inner_sum = jnp.sum(attention * grad_attention, axis=3, keepdims=True)
    grad_scores = (attention * (grad_attention - inner_sum)).astype(jnp.bfloat16)
    key_grads = jnp.einsum(
        "ehij,eihd->ejhd",
        grad_scores[:, :, :, :PTOK],
        query_heads,
        preferred_element_type=jnp.float32,
    )
    key_grads = (key_grads * score_scale).astype(jnp.bfloat16).reshape(examples, PTOK, D)
    value_grads = jnp.einsum(
        "ehij,eihd->ejhd",
        attention_rounded[:, :, :, :PTOK],
        cot_heads,
        preferred_element_type=jnp.float32,
    )
    value_grads = value_grads.astype(jnp.bfloat16).reshape(examples, PTOK, D)
    return (attended, jnp.stack([key_grads, value_grads], axis=2))


def tile_products(tile_grad, source_prompts, mix_weights, col_width):
    rows_here = tile_grad.shape[1]
    own_prompts = lax.dynamic_slice_in_dim(
        source_prompts, lax.axis_index("dp") * rows_here, rows_here, 1
    )
    tile_flat = tile_grad.reshape(NTASK, rows_here * col_width)
    source_grad = jnp.dot(mix_weights.T, tile_flat, precision=lax.Precision.HIGHEST)
    source_grad = source_grad.reshape(NSRC, rows_here, col_width)
    weight_part = jnp.dot(
        tile_flat,
        own_prompts.reshape(NSRC, rows_here * col_width).astype(jnp.float32).T,
        precision=lax.Precision.HIGHEST,
    )
    return (source_grad, weight_part)


def on_device(
    source_prompts,
    task_logits,
    task_ids,
    key_weight,
    value_weight,
    queries,
    keys,
    values,
    cotangent,
):
    col_width = key_weight.shape[1]
    group_examples = task_ids.shape[0]
    mix_weights = jax.nn.softmax(task_logits, axis=1)
    mix_rounded = mix_weights.astype(jnp.bfloat16)
    mixture = jnp.dot(
        mix_rounded,
        source_prompts.reshape(NSRC, PTOK * col_width),
        preferred_element_type=jnp.float32,
    )
    mixture = mixture.astype(jnp.bfloat16).reshape(NTASK, PTOK, col_width)
    pair_weight = jnp.concatenate([key_weight, value_weight], axis=1)
    portion = lax.all_gather(mixture, "mp", axis=2, tiled=True)
    portion_rows = portion.reshape(NTASK * PTOK, portion.shape[2])
    projected = jnp.dot(portion_rows, pair_weight, preferred_element_type=jnp.float32)
    projected = projected.astype(jnp.bfloat16).reshape(NTASK, PTOK, 2, col_width)
    task_range = jnp.arange(NTASK, dtype=jnp.int32)
    selector_all = (task_ids[:, None] == task_range[None, :]).astype(jnp.bfloat16)
    table_full = lax.all_gather(projected, "mp", axis=3, tiled=True)
    own_offset = lax.axis_index("mp") * E_DEV
    own_selector = lax.dynamic_slice_in_dim(selector_all, own_offset, E_DEV, 0)
    chosen = jnp.dot(
        own_selector, table_full.reshape(NTASK, PTOK * 2 * D), preferred_element_type=jnp.float32
    )
    prompt_pair = chosen.astype(jnp.bfloat16).reshape(E_DEV, PTOK, 2, D)
    attended, outgoing_grads = example_block(prompt_pair, queries, keys, values, cotangent)
    incoming = lax.all_to_all(outgoing_grads, "mp", split_axis=3, concat_axis=0, tiled=True)
    group_grads = jnp.dot(
        selector_all.T,
        incoming.reshape(group_examples, PTOK * 2 * col_width),
        preferred_element_type=jnp.float32,
    )
    pair_weight_t = pair_weight.astype(jnp.float32).T
    task_rows = lax.psum_scatter(
        group_grads.reshape(NTASK, PTOK, 2 * col_width), "dp", scatter_dimension=1, tiled=True
    )
    rows_here = task_rows.shape[1]
    row_terms = jnp.dot(
        task_rows.reshape(NTASK * rows_here, 2 * col_width),
        pair_weight_t,
        precision=lax.Precision.HIGHEST,
    ).reshape(NTASK, rows_here, D)
    tile_grad = lax.psum_scatter(row_terms, "mp", scatter_dimension=2, tiled=True)
    source_grad, weight_part = tile_products(tile_grad, source_prompts, mix_weights, col_width)
    weight_grad = lax.psum(weight_part, ("dp", "mp"))
    logits_grad = mix_weights * (
        weight_grad - jnp.sum(mix_weights * weight_grad, axis=1, keepdims=True)
    )
    return (attended, source_grad, logits_grad)


def solution(mesh):
    placed = (
        P(None, None, "mp"),
        P(),
        P("dp"),
        P(None, "mp"),
        P(None, "mp"),
        P(("dp", "mp"), None, None),
        P(("dp", "mp"), None, None),
        P(("dp", "mp"), None, None),
        P(("dp", "mp"), None, None),
    )
    return jax.shard_map(
        on_device,
        mesh=mesh,
        in_specs=placed,
        out_specs=(P(("dp", "mp"), None, None), P(None, "dp", "mp"), P()),
        check_vma=False,
    )
```

profile of v0, /device:TPU:0, one launch (start us, length us, event | category | flops | bytes accessed | tf_op | source)
XLA Modules:
  0.0 497.3 jit_solution(17414920822181697347)
XLA Ops:
  7.2 0.8 reduce_max.18
  8.0 0.9 fusion.44
  8.9 12.5 %copy.91 = bf16[16,8,64,512]{3,1,2,0:T(8,128)(2,1)} copy(bf16[16,8,64,512]{3,2,1,0:T(8,128)(2,1)} %bitcast.125) | data formatting | bytes 16777216
  21.4 4.6 convolution_convert_fusion
  26.0 1.0 copy.63
  27.0 4.7 constant_dynamic-update-slice_fusion.1
  31.7 2.3 constant_dynamic-update-slice_fusion
  34.0 70.5 %all-gather.3.cloned.1.call-done = bf16[8,64,4096]{2,1,0:T(8,128)(2,1)} async-done(((bf16[8,64,512]{2,1,0:T(8,128)(2,1)}), bf16[8,64,4096]{2,1,0:T(8,128)(2,1)}) %all-gather.3.cloned.1.call-update) | async-done | bytes 4194320 | tf_op jit(solution)/shard_map/all_gather | solution.py:104
  104.5 9.1 %convolution_convert_fusion.1 = bf16[512,1024]{1,0:T(8,128)(2,1)S(1)} fusion(bf16[512,4096]{1,0:T(8,128)(2,1)} %bitcast.147, bf16[4096,1024]{1,0:T(8,128)(2,1)} %constant_dynamic-update-slice_fusion), kind=kOutput, calls=%fused_computation.30 | convolution fusion | flops 4295491584 | bytes 13631488 | tf_op jit(solution)/shard_map/dot_general | solution.py:106
  113.7 1.6 reshape.180
  115.8 1.2 copy.94
  117.0 0.7 copy.67
  117.7 1.3 copy.69
  119.0 0.7 copy.64
  119.6 1.4 copy.73
  121.0 1.6 copy.95
  122.9 115.7 %all-gather.5.cloned.1.call-done = bf16[8,64,2,4096]{3,2,1,0:T(2,128)(2,1)} async-done(((bf16[8,64,2,512]{3,2,1,0:T(2,128)(2,1)}), bf16[8,64,2,4096]{3,2,1,0:T(2,128)(2,1)}) %all-gather.5.cloned.1.call-update) | async-done | bytes 8388624 | tf_op jit(solution)/shard_map/all_gather | solution.py:110
  238.5 13.0 %reshape.181 = bf16[8,524288]{1,0:T(8,128)(2,1)} reshape(bf16[8,64,2,4096]{3,2,1,0:T(2,128)(2,1)} %all-gather.5.cloned.1.call-done) | data formatting | bytes 16777216 | tf_op jit(solution)/shard_map/reshape | solution.py:114
  251.5 5.7 %fusion.46 = f32[1,524288]{1,0:T(1,128)S(1)} fusion(bf16[8,524288]{1,0:T(8,128)(2,1)} %reshape.181, pred[8,8]{1,0:T(8,128)(4,1)S(1)} %iota_compare_fusion.1, s32[]{:T(128)S(6)} %select_n.11), kind=kOutput, calls=%fused_computation.69 | convolution fusion | flops 8388608 | bytes 10486276 | tf_op jit(solution)/shard_map/dot_general | solution.py:113
  257.2 1.1 convert_element_type.64
  258.3 1.3 reshape.182
  259.7 5.6 %slice_reduce_fusion = (bf16[64,4096]{1,0:T(8,128)(2,1)S(1)}, bf16[64,4096]{1,0:T(8,128)(2,1)S(1)}) fusion(bf16[1,64,2,4096]{3,2,1,0:T(2,128)(2,1)S(1)} %reshape.182), kind=kLoop, calls=%fused_computation.40 | loop fusion | bytes 2097152 | tf_op jit(solution)/shard_map/slice | solution.py:22
  265.7 0.8 fusion.12
  266.6 0.9 fusion.57
  267.5 1.5 convert_bitcast_fusion
  269.5 0.9 fusion.15
  270.3 0.8 fusion.22
  272.3 1.6 fusion.26
  274.5 1.1 pad_maximum_fusion
  275.5 5.0 %copy.79 = bf16[1,64,2,4096]{1,2,0,3:T(2,128)(2,1)S(1)} copy(bf16[1,64,2,4096]{3,1,2,0:T(8,128)(2,1)} %pad_maximum_fusion) | data formatting | bytes 2097152 | tf_op jit(solution)/shard_map/stack | solution.py:63
  280.6 2.7 reshape.201
  283.2 29.5 %all_to_all.15 = bf16[8,2,32768]{2,1,0:T(2,128)(2,1)} all-to-all(bf16[8,2,32768]{2,1,0:T(2,128)(2,1)} %reshape.201), channel_id=1, replica_groups=mesh['dp'=4,'mp'=8] {'mp'}, dimensions={0} | all-to-all | bytes 2097152 | tf_op jit(solution)/shard_map/all_to_all | solution.py:118
  312.8 3.1 reshape.202
  315.9 3.6 copy.80
  319.5 2.0 reshape.190
  321.5 1.9 fusion.41
  323.7 30.1 %reduce-scatter.3.cloned.1.call-done = f32[8,16,1024]{2,0,1:T(8,128)} async-done(((f32[8,64,1024]{2,0,1:T(8,128)}), f32[8,16,1024]{2,0,1:T(8,128)}) %reduce-scatter.3.cloned.1.call-update) | async-done | bytes 524304 | tf_op jit(solution)/shard_map/reduce_scatter | solution.py:125
  353.8 13.3 %fusion.2 = f32[8,16,4096]{2,1,0:T(8,128)} fusion(bf16[4096,1024]{1,0:T(8,128)(2,1)} %constant_dynamic-update-slice_fusion, f32[8,16,1024]{2,0,1:T(8,128)} %reduce-scatter.3.cloned.1.call-done), kind=kOutput, calls=%fused_computation.3 | convolution fusion | flops 6442450944 | bytes 11010048 | tf_op jit(solution)/shard_map/dot_general | solution.py:129
  367.1 1.3 copy.66
  368.5 1.9 constant_dynamic-slice_fusion
  371.4 0.8 fusion.23
  372.3 1.3 copy.85
  373.6 62.6 %reduce-scatter.5.cloned.1.call-done = f32[8,16,512]{2,1,0:T(8,128)} async-done(((f32[8,16,4096]{2,1,0:T(8,128)}), f32[8,16,512]{2,1,0:T(8,128)}) %reduce-scatter.5.cloned.1.call-update) | async-done | bytes 262160 | tf_op jit(solution)/shard_map/reduce_scatter | solution.py:134
  436.2 4.6 fusion.28
  440.8 39.8 %psum.7 = f32[8,128]{1,0:T(8,128)S(1)} all-reduce(f32[8,128]{1,0:T(8,128)S(1)} %fusion.28), channel_id=1, replica_groups=mesh['dp'=4,'mp'=8] {'dp','mp'}, use_global_device_ids=true, to_apply=%region_7.8 | all-reduce | flops 1024 | bytes 8192 | tf_op jit(solution)/shard_map/psum | solution.py:136
  480.7 0.7 subtract_multiply_fusion
  481.4 4.5 fusion.39
  485.9 4.4 copy.86
  (51 shorter events, 4.9 us)
Async XLA Ops:
  7.2 97.3 %all-gather.3.cloned.1.call-start = ((), (), s32[]{:S(2)}) async-start(), calls=%async_computation.3 | async-start | bytes 4718592 | tf_op jit(solution)/shard_map/all_gather | solution.py:104
  8.9 12.5 %copy-start.12 = (f32[8,128]{1,0:T(8,128)S(1)}, f32[8,128]{1,0:T(8,128)}, u32[]{:S(2)}) copy-start(f32[8,128]{1,0:T(8,128)} %param.10) | copy-start | bytes 12292
  27.0 211.6 %all-gather.5.cloned.1.call-start = ((), (), s32[]{:S(2)}) async-start(), calls=%async_computation.4 | async-start | bytes 9437184 | tf_op jit(solution)/shard_map/all_gather | solution.py:110
  27.0 4.7 copy-start.2
  113.6 2.1 copy-start.8
  113.6 3.4 copy-start.9
  115.3 238.5 %reduce-scatter.3.cloned.1.call-start = ((), (), s32[]{:S(2)}) async-start(), calls=%async_computation.5 | async-start | bytes 2621440 | tf_op jit(solution)/shard_map/reduce_scatter | solution.py:125
  115.8 3.2 copy-start.10
  119.0 3.7 copy-start.13
  259.6 6.1 %copy-start.3 = (bf16[16,8,32,128]{3,2,1,0:T(8,128)(2,1)S(1)}, bf16[16,8,32,128]{3,2,1,0:T(8,128)(2,1)}, u32[]{:S(2)}) copy-start(bf16[16,8,32,128]{3,2,1,0:T(8,128)(2,1)} %copy.94) | copy-start | bytes 3145732
  259.6 6.1 %copy-start.5 = (bf16[1,128,32,128]{3,1,2,0:T(8,128)(2,1)S(1)}, bf16[1,128,32,128]{3,1,2,0:T(8,128)(2,1)}, u32[]{:S(2)}) copy-start(bf16[1,128,32,128]{3,1,2,0:T(8,128)(2,1)} %copy.69) | copy-start | bytes 3145732
  265.3 1.3 copy-start
  267.4 2.9 copy-start.6
  267.4 2.0 copy-start.4
  323.4 112.7 %reduce-scatter.5.cloned.1.call-start = ((), (), s32[]{:S(2)}) async-start(), calls=%async_computation.6 | async-start | bytes 2359296 | tf_op jit(solution)/shard_map/reduce_scatter | solution.py:134
  368.4 1.9 copy-start.1
  368.4 2.7 copy-start.7
  368.4 3.0 copy-start.11
Sparse Core Ops, SparseCore 0:
  27.1 77.3 all-gather.2
  115.4 123.1 all-gather.4
  323.6 30.1 reduce-scatter.2
  367.2 68.8 reduce-scatter.4
where the time goes:
time: 506 us; the launch traced here: 497 us
  waiting for transfers between devices  279 us (55%)
  local copies, waits for them, and re-layouts  77.2 us (15%)
  blocking collectives  69.3 us (14%)
  matrix products  48.4 us (10%)
  between operations  14.5 us (3%)
  other arithmetic  8.09 us (2%)
    all_gather x1, waiting for transfers between devices, on_device(): table_full = lax.all_gather(projected, 'mp', axis=3, tiled=True)  116 us
    all_gather x1, waiting for transfers between devices, on_device(): portion = lax.all_gather(mixture, 'mp', axis=2, tiled=True)  70.5 us
    reduce_scatter x1, waiting for transfers between devices, on_device(): lax.psum_scatter(row_terms, 'mp', scatter_dimension=2, tiled=True)  62.6 us
    psum x1, blocking collectives, on_device(): weight_grad = lax.psum(weight_part, ('dp', 'mp'))  39.8 us
    unnamed x40, local copies, waits for them, and re-layouts  34.1 us
    reduce_scatter x1, waiting for transfers between devices, on_device(): lax.psum_scatter(group_grads.reshape(NTASK, PTOK, 2 * col_width), 'dp', s...  30.1 us
    all_to_all x1, blocking collectives, on_device(): lax.all_to_all(outgoing_grads, 'mp', split_axis=3, concat_axis=0, tiled=T...  29.5 us
    dot_general x1, matrix products, on_device(): jnp.dot(task_rows.reshape(NTASK * rows_here, 2 * col_width), pair_weight_...  13.3 us
  transfers between devices with their start and end apart: 4, of which 4 were waited for; matrix products, arithmetic and copies ran while one was open for 4% of the time, Pallas kernels for 0%

commit v1 on v0

--- a/solution.py
+++ b/solution.py
@@ -1,6 +1,10 @@
+import functools
+
 import jax
 import jax.numpy as jnp
 from jax import lax
+from jax.experimental import pallas as pl
+from jax.experimental.pallas import tpu as pltpu
 from jax.sharding import PartitionSpec as P
 
 D = 4096
@@ -140,6 +144,386 @@
     return (attended, source_grad, logits_grad)
 
 
+BF = jnp.bfloat16
+F32 = jnp.float32
+
+
+def mm(a, b, ca=1, cb=0, precision=None):
+    return lax.dot_general(
+        a, b, (((ca,), (cb,)), ((), ())), preferred_element_type=F32, precision=precision
+    )
+
+
+def chain_kernel(
+    ndp, nmp,
+    logits, ids_in, sp_hbm, kw_hbm, vw_hbm, q_hbm, k_hbm, v_hbm, c_hbm,
+    att_out, tile_out, lg_out, w_out,
+    p_v, kw_v, vw_v, q_v, k_v, v_v, c_v,
+    mixed, ids_buf, sbuf, pair, gr, rbuf, ys, yr, zs, zr, wp, wbuf,
+    lsem, gs, gv, fs, fv, js, jv, bs, bv, cs, cv, us, uv, ts, tv, ws, wv,
+):
+    n = ndp * nmp
+    nz = nmp // 2
+    width = kw_v.shape[1]
+    rows = p_v.shape[1]
+    nsrc = p_v.shape[0]
+    ntask = logits.shape[0]
+    tp = ntask * rows
+    spn = nsrc * rows
+    seq = q_v.shape[0]
+    d = lax.axis_index("dp")
+    m = lax.axis_index("mp")
+    z = m // 2
+    y = m % 2
+    me = d * nmp + m
+    other = z * 2 + (1 - y)
+
+    def remote(src, dst, ss, rs, dd, mm_):
+        return pltpu.make_async_remote_copy(
+            src_ref=src, dst_ref=dst, send_sem=ss, recv_sem=rs,
+            device_id=(dd, mm_), device_id_type=pl.DeviceIdType.MESH,
+        )
+
+    barrier = pltpu.get_barrier_semaphore()
+
+    @pl.loop(1, n)
+    def _(k):
+        to = lax.rem(me + k, n)
+        pl.semaphore_signal(
+            barrier, inc=1, device_id=(to // nmp, lax.rem(to, nmp)),
+            device_id_type=pl.DeviceIdType.MESH,
+        )
+
+    loads = [
+        pltpu.make_async_copy(
+            sp_hbm.at[:, pl.ds(pl.multiple_of(d * rows, rows), rows), :], p_v, lsem.at[0]
+        )
+    ]
+    for i, (a, b) in enumerate(
+        ((kw_hbm, kw_v), (vw_hbm, vw_v), (k_hbm, k_v), (q_hbm, q_v), (v_hbm, v_v), (c_hbm, c_v))
+    ):
+        loads.append(pltpu.make_async_copy(a, b, lsem.at[1 + i]))
+    for c in loads:
+        c.start()
+
+    lg = logits[...]
+    ex = jnp.exp(lg - jnp.max(lg, axis=1, keepdims=True))
+    mix = ex / jnp.sum(ex, axis=1, keepdims=True)
+    up = (
+        lax.broadcasted_iota(jnp.int32, (tp, ntask), 0) // rows
+        == lax.broadcasted_iota(jnp.int32, (tp, ntask), 1)
+    )
+    tall = mm(jnp.where(up, 1.0, 0.0), mix.astype(BF).astype(F32)).astype(BF)
+    out = (
+        lax.broadcasted_iota(jnp.int32, (nsrc, spn), 1) // rows
+        == lax.broadcasted_iota(jnp.int32, (nsrc, spn), 0)
+    )
+    wide = mm(tall, jnp.where(out, 1.0, 0.0).astype(BF))
+    same = (
+        lax.broadcasted_iota(jnp.int32, (tp, spn), 0) % rows
+        == lax.broadcasted_iota(jnp.int32, (tp, spn), 1) % rows
+    )
+    w_out[...] = jnp.where(same, wide, 0.0).astype(BF)
+    ids_buf[d] = ids_in[...]
+
+    loads[0].wait()
+    mixed[m] = mm(w_out[...], p_v[...].reshape(spn, width)).astype(BF)
+
+    pl.semaphore_wait(barrier, n - 1)
+
+    idc = []
+    for j in range(1, ndp):
+        c = remote(ids_in, ids_buf.at[d], js.at[j], jv.at[j], lax.rem(d + j, ndp), m)
+        c.start()
+        idc.append(c)
+    gat = []
+    for j in range(1, nz):
+        c = remote(
+            mixed.at[m], mixed.at[m], gs.at[j], gv.at[j], d, lax.rem(z + j, nz) * 2 + y
+        )
+        c.start()
+        gat.append(c)
+    fwd = [remote(mixed.at[m], mixed.at[m], fs.at[0], fv.at[0], d, other)]
+    fwd[0].start()
+    for c in idc:
+        c.wait()
+    loads[1].wait()
+    loads[2].wait()
+
+    def part(slot):
+        block = mixed[slot]
+        at = pl.ds(pl.multiple_of(slot * width, width), width)
+        return mm(block, kw_v[at, :]), mm(block, vw_v[at, :])
+
+    pk, pv = part(m)
+    for j in range(1, nz):
+        slot = lax.rem(z + nz - j, nz) * 2 + y
+        gat[j - 1].wait_recv()
+        c = remote(mixed.at[slot], mixed.at[slot], fs.at[j], fv.at[j], d, other)
+        c.start()
+        fwd.append(c)
+        a, b = part(slot)
+        pk, pv = pk + a, pv + b
+    for j in range(nz):
+        slot = lax.rem(z + nz - j, nz) * 2 + (1 - y)
+        fwd[j].wait_recv()
+        a, b = part(slot)
+        pk, pv = pk + a, pv + b
+
+    ids_all = ids_buf[...].reshape(n, tp).astype(BF)
+    rep = (
+        lax.broadcasted_iota(jnp.int32, (n * rows, n), 0) // rows
+        == lax.broadcasted_iota(jnp.int32, (n * rows, n), 1)
+    )
+    ids_x = mm(jnp.where(rep, 1.0, 0.0).astype(BF), ids_all)
+    lane = lax.broadcasted_iota(jnp.int32, (n * rows, tp), 1)
+    row = lax.broadcasted_iota(jnp.int32, (n * rows, tp), 0)
+    sel = jnp.where(
+        (ids_x == (lane // rows).astype(F32)) & (lane % rows == row % rows), 1.0, 0.0
+    ).astype(BF)
+    sbuf[:, 0] = mm(sel, pk.astype(BF)).astype(BF).reshape(n, rows, width)
+    sbuf[:, 1] = mm(sel, pv.astype(BF)).astype(BF).reshape(n, rows, width)
+
+    my_rows = pl.ds(pl.multiple_of(d * rows, rows), rows)
+    my_cols = pl.ds(pl.multiple_of(m * width, width), width)
+
+    def b_copy(k):
+        dd, gg = lax.rem(k, ndp), k // ndp
+        td, tm = lax.rem(d + ndp - dd, ndp), lax.rem(m + nmp - gg, nmp)
+        return remote(
+            sbuf.at[td * nmp + tm], pair.at[:, my_rows, my_cols], bs.at[k], bv.at[k], td, tm
+        )
+
+    own_b = pltpu.make_async_copy(sbuf.at[me], pair.at[:, my_rows, my_cols], lsem.at[7])
+    own_b.start()
+
+    @pl.loop(1, n)
+    def _(k):
+        b_copy(k).start()
+
+    for c in loads[3:]:
+        c.wait()
+    own_b.wait()
+
+    def c_copy(k):
+        dd, gg = lax.rem(k, ndp), k // ndp
+        td, tm = lax.rem(d + dd, ndp), lax.rem(m + gg, nmp)
+        return remote(
+            gr.at[
+                :,
+                pl.ds(pl.multiple_of(td * rows, rows), rows),
+                pl.ds(pl.multiple_of(tm * width, width), width),
+            ],
+            rbuf.at[me], cs.at[k], cv.at[k], td, tm,
+        )
+
+    scale = DH ** (-0.5)
+    seen = lax.broadcasted_iota(jnp.int32, (seq, seq), 1) <= lax.broadcasted_iota(
+        jnp.int32, (seq, seq), 0
+    )
+
+    def group(g, wait_from):
+        @pl.loop(wait_from, ndp)
+        def _(dd):
+            b_copy(g * ndp + dd).wait_recv()
+
+        base = lax.rem(m + g, nmp) * width
+        for h in range(width // DH):
+            at = pl.ds(pl.multiple_of(base + h * DH, DH), DH)
+            q, c, kk, vv = q_v[:, at], c_v[:, at], k_v[:, at], v_v[:, at]
+            kp, vp = pair[0, :, at], pair[1, :, at]
+            s1 = mm(q, kp, 1, 1) * scale
+            s2 = jnp.where(seen, mm(q, kk, 1, 1) * scale, mask_fill)
+            top = jnp.maximum(
+                jnp.max(s1, axis=1, keepdims=True), jnp.max(s2, axis=1, keepdims=True)
+            )
+            e1, e2 = jnp.exp(s1 - top), jnp.exp(s2 - top)
+            inv = 1.0 / (
+                jnp.sum(e1, axis=1, keepdims=True) + jnp.sum(e2, axis=1, keepdims=True)
+            )
+            a1, a2 = e1 * inv, e2 * inv
+            b1 = a1.astype(BF)
+            att_out[:, at] = (mm(b1, vp) + mm(a2.astype(BF), vv)).astype(BF)
+            g1, g2 = mm(c, vp, 1, 1), mm(c, vv, 1, 1)
+            inner = jnp.sum(a1 * g1, axis=1, keepdims=True) + jnp.sum(
+                a2 * g2, axis=1, keepdims=True
+            )
+            gs1 = (a1 * (g1 - inner)).astype(BF)
+            gr[0, :, at] = (mm(gs1, q, 0, 0) * scale).astype(BF)
+            gr[1, :, at] = mm(b1, c, 0, 0).astype(BF)
+
+    group(0, 1)
+    own_c = pltpu.make_async_copy(gr.at[:, my_rows, my_cols], rbuf.at[me], lsem.at[8])
+    own_c.start()
+
+    @pl.loop(1, ndp)
+    def _(dd):
+        c_copy(dd).start()
+
+    @pl.loop(1, nmp)
+    def _(g):
+        group(g, 0)
+
+        @pl.loop(0, ndp)
+        def _(dd):
+            c_copy(g * ndp + dd).start()
+
+    own_c.wait()
+
+    @pl.loop(1, n)
+    def _(k):
+        c_copy(k).wait_recv()
+
+    tk = mm(sel, rbuf[:, 0].reshape(n * rows, width), 0, 0).astype(BF)
+    tv_ = mm(sel, rbuf[:, 1].reshape(n * rows, width), 0, 0).astype(BF)
+
+    def term(slot):
+        at = pl.ds(pl.multiple_of(slot * width, width), width)
+        return mm(tk, kw_v[at, :], 1, 1) + mm(tv_, vw_v[at, :], 1, 1)
+
+    yc, zc = [None] * nz, [None] * nz
+    order = list(range(1, nz)) + [0]
+    for j in order:
+        ys[j] = term(lax.rem(z + j, nz) * 2 + (1 - y)).astype(BF)
+        yc[j] = remote(ys.at[j], yr.at[j], us.at[j], uv.at[j], d, other)
+        yc[j].start()
+    for j in order:
+        to = lax.rem(z + j, nz) * 2 + y
+        mine = term(to)
+        yc[j].wait_recv()
+        mine = mine + yr[j].astype(F32)
+        if j:
+            zs[j] = mine.astype(BF)
+            zc[j] = remote(zs.at[j], zr.at[j], ts.at[j], tv.at[j], d, to)
+            zc[j].start()
+    for j in range(1, nz):
+        zc[j].wait_recv()
+        mine = mine + zr[j].astype(F32)
+    tile = mine.astype(BF)
+    tile_out[...] = tile
+
+    prod = mm(p_v[...].reshape(spn, width), tile, 1, 1)
+    same_t = (
+        lax.broadcasted_iota(jnp.int32, (spn, tp), 0) % rows
+        == lax.broadcasted_iota(jnp.int32, (spn, tp), 1) % rows
+    )
+    prod = jnp.sum(jnp.where(same_t, prod, 0.0).reshape(nsrc, rows, tp), axis=1)
+    fold = (
+        lax.broadcasted_iota(jnp.int32, (ntask, tp), 1) // rows
+        == lax.broadcasted_iota(jnp.int32, (ntask, tp), 0)
+    )
+    part_w = mm(jnp.where(fold, 1.0, 0.0), prod, 1, 1, lax.Precision.HIGHEST)
+    wp[...] = part_w
+    wbuf[me] = part_w
+
+    def w_copy(k):
+        to = lax.rem(me + k, n)
+        return remote(wp, wbuf.at[me], ws.at[k], wv.at[k], to // nmp, lax.rem(to, nmp))
+
+    @pl.loop(1, n)
+    def _(k):
+        w_copy(k).start()
+
+    for c in idc + gat + fwd:
+        pass
+    for c in gat + fwd + yc + zc[1:]:
+        c.wait_send()
+
+    @pl.loop(1, n)
+    def _(k):
+        b_copy(k).wait_send()
+        c_copy(k).wait_send()
+
+    @pl.loop(1, n)
+    def _(k):
+        w_copy(k).wait()
+
+    wg = jnp.sum(wbuf[...], axis=0)
+    lg_out[...] = mix * (wg - jnp.sum(mix * wg, axis=1, keepdims=True))
+
+
+def source_kernel(w_ref, tile_ref, out_ref):
+    got = mm(w_ref[...], tile_ref[...], 0, 0)
+    out_ref[...] = got.reshape(out_ref.shape)
+
+
+def per_device(ndp, nmp, *args):
+    source_prompts, task_logits, task_ids, key_weight, value_weight = args[:5]
+    queries, keys, values, cotangent = args[5:]
+    nsrc, ptok, width = source_prompts.shape
+    ntask = task_logits.shape[0]
+    ge = task_ids.shape[0]
+    rows = ptok // ndp
+    if width % DH or nmp % 2 or ge != nmp or ptok % ndp or rows % 16 or ntask * rows != 128:
+        return on_device(*args)
+    n, nz = ndp * nmp, nmp // 2
+    tp, spn = ntask * rows, nsrc * rows
+    seq, full = queries.shape[1:]
+    ids_tile = jnp.broadcast_to(task_ids.astype(F32)[:, None], (ge, tp))
+    vmem = pl.BlockSpec(memory_space=pltpu.VMEM)
+    hbm = pl.BlockSpec(memory_space=pl.ANY)
+    dma = pltpu.SemaphoreType.DMA
+    attended, tile, logits_grad, w_big = pl.pallas_call(
+        functools.partial(chain_kernel, ndp, nmp),
+        out_shape=(
+            jax.ShapeDtypeStruct((seq, full), BF),
+            jax.ShapeDtypeStruct((tp, width), BF),
+            jax.ShapeDtypeStruct((ntask, nsrc), F32),
+            jax.ShapeDtypeStruct((tp, spn), BF),
+        ),
+        in_specs=[vmem, vmem] + [hbm] * 7,
+        out_specs=(vmem,) * 4,
+        scratch_shapes=[
+            pltpu.VMEM((nsrc, rows, width), BF),
+            pltpu.VMEM((full, width), BF),
+            pltpu.VMEM((full, width), BF),
+            pltpu.VMEM((seq, full), BF),
+            pltpu.VMEM((seq, full), BF),
+            pltpu.VMEM((seq, full), BF),
+            pltpu.VMEM((seq, full), BF),
+            pltpu.VMEM((nmp, tp, width), BF),
+            pltpu.VMEM((ndp, ge, tp), F32),
+            pltpu.VMEM((n, 2, rows, width), BF),
+            pltpu.VMEM((2, ptok, full), BF),
+            pltpu.VMEM((2, ptok, full), BF),
+            pltpu.VMEM((n, 2, rows, width), BF),
+            pltpu.VMEM((nz, tp, width), BF),
+            pltpu.VMEM((nz, tp, width), BF),
+            pltpu.VMEM((nz, tp, width), BF),
+            pltpu.VMEM((nz, tp, width), BF),
+            pltpu.VMEM((ntask, nsrc), F32),
+            pltpu.VMEM((n, ntask, nsrc), F32),
+            dma((9,)),
+            dma((nz,)), dma((nz,)), dma((nz,)), dma((nz,)),
+            dma((ndp,)), dma((ndp,)),
+            dma((n,)), dma((n,)), dma((n,)), dma((n,)),
+            dma((nz,)), dma((nz,)), dma((nz,)), dma((nz,)),
+            dma((n,)), dma((n,)),
+        ],
+        compiler_params=pltpu.CompilerParams(
+            collective_id=0, has_side_effects=True, vmem_limit_bytes=60 * 2**20
+        ),
+        name="chain",
+    )(
+        task_logits, ids_tile, source_prompts, key_weight, value_weight,
+        queries.reshape(seq, full), keys.reshape(seq, full),
+        values.reshape(seq, full), cotangent.reshape(seq, full),
+    )
+    steps = 8
+    source_grad = pl.pallas_call(
+        source_kernel,
+        grid=(steps,),
+        out_shape=jax.ShapeDtypeStruct((nsrc, rows, width), F32),
+        in_specs=[
+            pl.BlockSpec((tp, spn // steps), lambda i: (0, i)),
+            pl.BlockSpec((tp, width), lambda i: (0, 0)),
+        ],
+        out_specs=pl.BlockSpec((nsrc // steps, rows, width), lambda i: (i, 0, 0)),
+        name="source_grad",
+    )(w_big, tile)
+    return (attended.reshape(queries.shape), source_grad, logits_grad)
+
+
 def solution(mesh):
     placed = (
         P(None, None, "mp"),
@@ -153,7 +537,7 @@
         P(("dp", "mp"), None, None),
     )
     return jax.shard_map(
-        on_device,
+        functools.partial(per_device, mesh.shape["dp"], mesh.shape["mp"]),
         mesh=mesh,
         in_specs=placed,
         out_specs=(P(("dp", "mp"), None, None), P(None, "dp", "mp"), P()),

time: 506 us -> 112 us (0.22); the launches traced: 497 us -> 112 us
  waiting for transfers between devices: 279 us -> 0 us
  Pallas kernels: 0 us -> 108 us
  local copies, waits for them, and re-layouts: 77.2 us -> 2.23 us
  blocking collectives: 69.3 us -> 0 us
  matrix products: 48.4 us -> 0 us
  between operations: 14.5 us -> 0.66 us
  other arithmetic: 8.09 us -> 0.66 us
    all_gather x2 -> x0, waiting for transfers between devices: 186 us -> none  [the longest x1 116 us: on_device(): table_full = lax.all_gather(projected, 'mp', axis=3, tiled=True)]
    pallas_call x0 -> x2, Pallas kernels: none -> 108 us  [the longest x1 102 us: per_device(): pl.pallas_call(functools.partial(chain_kernel, ndp, nmp), out_shape=(jax....]
    reduce_scatter x2 -> x0, waiting for transfers between devices: 92.7 us -> none  [the longest x1 62.6 us: on_device(): lax.psum_scatter(row_terms, 'mp', scatter_dimension=2, tiled=True)]
    dot_general x12 -> x0, matrix products: 48.4 us -> none  [the longest x1 13.3 us: on_device(): jnp.dot(task_rows.reshape(NTASK * rows_here, 2 * col_width), pair_weight_...]
    psum x1 -> x0, blocking collectives: 39.8 us -> none  [on_device(): weight_grad = lax.psum(weight_part, ('dp', 'mp'))]
    unnamed x40 -> x6, local copies, waits for them, and re-layouts: 34.1 us -> 1.57 us
    all_to_all x1 -> x0, blocking collectives: 29.5 us -> none  [on_device(): lax.all_to_all(outgoing_grads, 'mp', split_axis=3, concat_axis=0, tiled=T...]
    reshape x5 -> x0, local copies, waits for them, and re-layouts: 18.9 us -> none  [the longest x1 13 us: on_device(): table_full.reshape(NTASK, PTOK * 2 * D)]
  transfers between devices with their start and end apart: 4 -> 0, of which waited for: 4 -> 0; matrix products, arithmetic and copies ran while one was open for 4% -> 0% of each run, Pallas kernels for 0% -> 0%
where the time goes in v1:
time: 112 us
  Pallas kernels  108 us (96%)
  local copies, waits for them, and re-layouts  2.23 us (2%)
    pallas_call x1, Pallas kernels, per_device(): pl.pallas_call(functools.partial(chain_kernel, ndp, nmp), out_shape=(jax....  102 us
    pallas_call x1, Pallas kernels, per_device(): pl.pallas_call(source_kernel, grid=(steps,), out_shape=jax.ShapeDtypeStru...  6.37 us

profile of v1, /device:TPU:0, one launch (start us, length us, event | category | flops | bytes accessed | tf_op | source)
XLA Modules:
  0.0 112.0 jit_solution(15502123896237478138)
XLA Ops:
  0.6 0.7 convert_element_type.3
  1.3 0.7 broadcast_in_dim.2.ids_in
  2.0 102.1 %chain.1 = (bf16[128,4096]{1,0:T(8,128)(2,1)}, bf16[128,512]{1,0:T(8,128)(2,1)}, f32[8,128]{1,0:T(8,128)}, bf16[128,2048]{1,0:T(8,128)(2,1)}) custom-call(f32[8,128]{1,0:T(8,128)} %logits.1, f32[8,128]{1,0:T(8,128)} %broadcast_in_dim.2.ids_in, bf16[128,64,512]{2,1,0:T(8,128)(2,1)} %sp_hbm.1, bf16[4096,512]{1,0:T(8,128)(2,1)} %kw_hbm.1, ...), custom_call_target="tpu_custom_call" | custom-call | tf_op jit(solution)/shard_map/chain/pallas_call | solution.py:466
  104.0 0.0 copy-start
  104.0 0.0 copy-start.1
  104.0 6.4 %source_grad.1 = f32[128,16,512]{2,1,0:T(8,128)} custom-call(bf16[128,2048]{1,0:T(8,128)(2,1)} %get-tuple-element.8.w_ref, bf16[128,512]{1,0:T(8,128)(2,1)} %get-tuple-element.9.tile_ref), custom_call_target="tpu_custom_call" | custom-call | tf_op jit(solution)/shard_map/source_grad/pallas_call | solution.py:513
  110.4 0.0 copy-done
  110.4 1.0 copy.14
  111.4 0.0 copy-done.1
  111.4 0.6 copy.15
Async XLA Ops:
  104.0 6.4 %copy-start = (bf16[128,4096]{1,0:T(8,128)(2,1)S(1)}, bf16[128,4096]{1,0:T(8,128)(2,1)}, u32[]{:S(2)}) copy-start(bf16[128,4096]{1,0:T(8,128)(2,1)} %get-tuple-element.7) | copy-start | bytes 3145732
  104.0 7.4 %copy-start.1 = (f32[8,128]{1,0:T(8,128)S(1)}, f32[8,128]{1,0:T(8,128)}, u32[]{:S(2)}) copy-start(f32[8,128]{1,0:T(8,128)} %get-tuple-element.16) | copy-start | bytes 12292

commit v2 on v1

--- a/solution.py
+++ b/solution.py
@@ -159,7 +159,7 @@
     logits, ids_in, sp_hbm, kw_hbm, vw_hbm, q_hbm, k_hbm, v_hbm, c_hbm,
     att_out, tile_out, lg_out, w_out,
     p_v, kw_v, vw_v, q_v, k_v, v_v, c_v,
-    mixed, ids_buf, sbuf, pair, gr, rbuf, ys, yr, zs, zr, wp, wbuf,
+    mixed, ids_own, ids_buf, sbuf, pair, gr, rbuf, ys, yr, zs, zr, wp, wbuf,
     lsem, gs, gv, fs, fv, js, jv, bs, bv, cs, cv, us, uv, ts, tv, ws, wv,
 ):
     n = ndp * nmp
@@ -178,6 +178,17 @@
     me = d * nmp + m
     other = z * 2 + (1 - y)
 
+    shift = rows.bit_length() - 1
+
+    def iota(shape, axis):
+        return lax.broadcasted_iota(jnp.int32, shape, axis)
+
+    def outer(a):
+        return lax.shift_right_logical(a, jnp.int32(shift))
+
+    def same_row(shape):
+        return ((iota(shape, 0) ^ iota(shape, 1)) & (rows - 1)) == 0
+
     def remote(src, dst, ss, rs, dd, mm_):
         return pltpu.make_async_remote_copy(
             src_ref=src, dst_ref=dst, send_sem=ss, recv_sem=rs,
@@ -203,37 +214,35 @@
         ((kw_hbm, kw_v), (vw_hbm, vw_v), (k_hbm, k_v), (q_hbm, q_v), (v_hbm, v_v), (c_hbm, c_v))
     ):
         loads.append(pltpu.make_async_copy(a, b, lsem.at[1 + i]))
-    for c in loads:
-        c.start()
+    loads[0].start()
 
     lg = logits[...]
     ex = jnp.exp(lg - jnp.max(lg, axis=1, keepdims=True))
     mix = ex / jnp.sum(ex, axis=1, keepdims=True)
     up = (
-        lax.broadcasted_iota(jnp.int32, (tp, ntask), 0) // rows
-        == lax.broadcasted_iota(jnp.int32, (tp, ntask), 1)
+        outer(iota((tp, ntask), 0)) == iota((tp, ntask), 1)
     )
     tall = mm(jnp.where(up, 1.0, 0.0), mix.astype(BF).astype(F32)).astype(BF)
     out = (
-        lax.broadcasted_iota(jnp.int32, (nsrc, spn), 1) // rows
-        == lax.broadcasted_iota(jnp.int32, (nsrc, spn), 0)
+        outer(iota((nsrc, spn), 1)) == iota((nsrc, spn), 0)
     )
     wide = mm(tall, jnp.where(out, 1.0, 0.0).astype(BF))
-    same = (
-        lax.broadcasted_iota(jnp.int32, (tp, spn), 0) % rows
-        == lax.broadcasted_iota(jnp.int32, (tp, spn), 1) % rows
-    )
-    w_out[...] = jnp.where(same, wide, 0.0).astype(BF)
-    ids_buf[d] = ids_in[...]
+    w_out[...] = jnp.where(same_row((tp, spn)), wide, 0.0).astype(BF)
+    for j in range(ids_in.shape[0]):
+        line = jnp.full((1, tp), ids_in[j], jnp.int32).astype(F32)
+        ids_own[pl.ds(j, 1), :] = line
+        ids_buf[d, pl.ds(j, 1), :] = line
 
     loads[0].wait()
+    for c in loads[1:]:
+        c.start()
     mixed[m] = mm(w_out[...], p_v[...].reshape(spn, width)).astype(BF)
 
     pl.semaphore_wait(barrier, n - 1)
 
     idc = []
     for j in range(1, ndp):
-        c = remote(ids_in, ids_buf.at[d], js.at[j], jv.at[j], lax.rem(d + j, ndp), m)
+        c = remote(ids_own, ids_buf.at[d], js.at[j], jv.at[j], lax.rem(d + j, ndp), m)
         c.start()
         idc.append(c)
     gat = []
@@ -272,14 +281,11 @@
 
     ids_all = ids_buf[...].reshape(n, tp).astype(BF)
     rep = (
-        lax.broadcasted_iota(jnp.int32, (n * rows, n), 0) // rows
-        == lax.broadcasted_iota(jnp.int32, (n * rows, n), 1)
+        outer(iota((n * rows, n), 0)) == iota((n * rows, n), 1)
     )
     ids_x = mm(jnp.where(rep, 1.0, 0.0).astype(BF), ids_all)
-    lane = lax.broadcasted_iota(jnp.int32, (n * rows, tp), 1)
-    row = lax.broadcasted_iota(jnp.int32, (n * rows, tp), 0)
     sel = jnp.where(
-        (ids_x == (lane // rows).astype(F32)) & (lane % rows == row % rows), 1.0, 0.0
+        (ids_x == outer(iota((n * rows, tp), 1)).astype(F32)) & same_row((n * rows, tp)), 1.0, 0.0
     ).astype(BF)
     sbuf[:, 0] = mm(sel, pk.astype(BF)).astype(BF).reshape(n, rows, width)
     sbuf[:, 1] = mm(sel, pv.astype(BF)).astype(BF).reshape(n, rows, width)
@@ -318,9 +324,9 @@
         )
 
     scale = DH ** (-0.5)
-    seen = lax.broadcasted_iota(jnp.int32, (seq, seq), 1) <= lax.broadcasted_iota(
-        jnp.int32, (seq, seq), 0
-    )
+    to_exp2 = scale * 1.4426950408889634
+    ptok = pair.shape[1]
+    seen = iota((seq, seq), 0) <= iota((seq, seq), 1)
 
     def group(g, wait_from):
         @pl.loop(wait_from, ndp)
@@ -328,29 +334,26 @@
             b_copy(g * ndp + dd).wait_recv()
 
         base = lax.rem(m + g, nmp) * width
+        ats, st, gt, va = [], [], [], []
         for h in range(width // DH):
             at = pl.ds(pl.multiple_of(base + h * DH, DH), DH)
-            q, c, kk, vv = q_v[:, at], c_v[:, at], k_v[:, at], v_v[:, at]
-            kp, vp = pair[0, :, at], pair[1, :, at]
-            s1 = mm(q, kp, 1, 1) * scale
-            s2 = jnp.where(seen, mm(q, kk, 1, 1) * scale, mask_fill)
-            top = jnp.maximum(
-                jnp.max(s1, axis=1, keepdims=True), jnp.max(s2, axis=1, keepdims=True)
-            )
-            e1, e2 = jnp.exp(s1 - top), jnp.exp(s2 - top)
-            inv = 1.0 / (
-                jnp.sum(e1, axis=1, keepdims=True) + jnp.sum(e2, axis=1, keepdims=True)
-            )
-            a1, a2 = e1 * inv, e2 * inv
-            b1 = a1.astype(BF)
-            att_out[:, at] = (mm(b1, vp) + mm(a2.astype(BF), vv)).astype(BF)
-            g1, g2 = mm(c, vp, 1, 1), mm(c, vv, 1, 1)
-            inner = jnp.sum(a1 * g1, axis=1, keepdims=True) + jnp.sum(
-                a2 * g2, axis=1, keepdims=True
-            )
-            gs1 = (a1 * (g1 - inner)).astype(BF)
-            gr[0, :, at] = (mm(gs1, q, 0, 0) * scale).astype(BF)
-            gr[1, :, at] = mm(b1, c, 0, 0).astype(BF)
+            ats.append(at)
+            ka = jnp.concatenate([pair[0, :, at], k_v[:, at]], axis=0)
+            va.append(jnp.concatenate([pair[1, :, at], v_v[:, at]], axis=0))
+            st.append(mm(ka, q_v[:, at], 1, 1))
+            gt.append(mm(va[h], c_v[:, at], 1, 1))
+        for h in range(width // DH):
+            at = ats[h]
+            s = st[h] * to_exp2
+            s = jnp.concatenate([s[:ptok], jnp.where(seen, s[ptok:], mask_fill)], axis=0)
+            e = jnp.exp2(s - jnp.max(s, axis=0, keepdims=True))
+            a = e * (1.0 / jnp.sum(e, axis=0, keepdims=True))
+            ab = a.astype(BF)
+            inner = jnp.sum(a * gt[h], axis=0, keepdims=True)
+            gs1 = (a[:ptok] * (gt[h][:ptok] - inner)).astype(BF)
+            gr[0, :, at] = (mm(gs1, q_v[:, at]) * scale).astype(BF)
+            gr[1, :, at] = mm(ab[:ptok], c_v[:, at]).astype(BF)
+            att_out[:, at] = mm(ab, va[h], 0, 0).astype(BF)
 
     group(0, 1)
     own_c = pltpu.make_async_copy(gr.at[:, my_rows, my_cols], rbuf.at[me], lsem.at[8])
@@ -403,14 +406,9 @@
     tile_out[...] = tile
 
     prod = mm(p_v[...].reshape(spn, width), tile, 1, 1)
-    same_t = (
-        lax.broadcasted_iota(jnp.int32, (spn, tp), 0) % rows
-        == lax.broadcasted_iota(jnp.int32, (spn, tp), 1) % rows
-    )
-    prod = jnp.sum(jnp.where(same_t, prod, 0.0).reshape(nsrc, rows, tp), axis=1)
+    prod = jnp.sum(jnp.where(same_row((spn, tp)), prod, 0.0).reshape(nsrc, rows, tp), axis=1)
     fold = (
-        lax.broadcasted_iota(jnp.int32, (ntask, tp), 1) // rows
-        == lax.broadcasted_iota(jnp.int32, (ntask, tp), 0)
+        outer(iota((ntask, tp), 1)) == iota((ntask, tp), 0)
     )
     part_w = mm(jnp.where(fold, 1.0, 0.0), prod, 1, 1, lax.Precision.HIGHEST)
     wp[...] = part_w
@@ -424,8 +422,6 @@
     def _(k):
         w_copy(k).start()
 
-    for c in idc + gat + fwd:
-        pass
     for c in gat + fwd + yc + zc[1:]:
         c.wait_send()
 
@@ -454,12 +450,11 @@
     ntask = task_logits.shape[0]
     ge = task_ids.shape[0]
     rows = ptok // ndp
-    if width % DH or nmp % 2 or ge != nmp or ptok % ndp or rows % 16 or ntask * rows != 128:
+    if width % DH or nmp % 2 or ge != nmp or ptok % ndp or rows % 16 or rows & (rows - 1) or ntask * rows != 128:
         return on_device(*args)
     n, nz = ndp * nmp, nmp // 2
     tp, spn = ntask * rows, nsrc * rows
     seq, full = queries.shape[1:]
-    ids_tile = jnp.broadcast_to(task_ids.astype(F32)[:, None], (ge, tp))
     vmem = pl.BlockSpec(memory_space=pltpu.VMEM)
     hbm = pl.BlockSpec(memory_space=pl.ANY)
     dma = pltpu.SemaphoreType.DMA
@@ -471,7 +466,7 @@
             jax.ShapeDtypeStruct((ntask, nsrc), F32),
             jax.ShapeDtypeStruct((tp, spn), BF),
         ),
-        in_specs=[vmem, vmem] + [hbm] * 7,
+        in_specs=[vmem, pl.BlockSpec(memory_space=pltpu.SMEM)] + [hbm] * 7,
         out_specs=(vmem,) * 4,
         scratch_shapes=[
             pltpu.VMEM((nsrc, rows, width), BF),
@@ -482,6 +477,7 @@
             pltpu.VMEM((seq, full), BF),
             pltpu.VMEM((seq, full), BF),
             pltpu.VMEM((nmp, tp, width), BF),
+            pltpu.VMEM((ge, tp), F32),
             pltpu.VMEM((ndp, ge, tp), F32),
             pltpu.VMEM((n, 2, rows, width), BF),
             pltpu.VMEM((2, ptok, full), BF),
@@ -505,11 +501,11 @@
         ),
         name="chain",
     )(
-        task_logits, ids_tile, source_prompts, key_weight, value_weight,
+        task_logits, task_ids, source_prompts, key_weight, value_weight,
         queries.reshape(seq, full), keys.reshape(seq, full),
         values.reshape(seq, full), cotangent.reshape(seq, full),
     )
-    steps = 8
+    steps = 4
     source_grad = pl.pallas_call(
         source_kernel,
         grid=(steps,),

time: 112 us -> 109 us (0.973)
    pallas_call x1, Pallas kernels: 6.37 us -> 4.56 us  [per_device(): pl.pallas_call(source_kernel, grid=(steps,), out_shape=jax.ShapeDtypeStru...]
where the time goes in v2:
time: 109 us
  Pallas kernels  107 us (98%)
  local copies, waits for them, and re-layouts  1.57 us (1%)
    pallas_call x1, Pallas kernels, per_device(): pl.pallas_call(functools.partial(chain_kernel, ndp, nmp), out_shape=(jax....  102 us
    pallas_call x1, Pallas kernels, per_device(): pl.pallas_call(source_kernel, grid=(steps,), out_shape=jax.ShapeDtypeStru...  4.56 us

profile of v2, /device:TPU:0, one launch (start us, length us, event | category | flops | bytes accessed | tf_op | source)
XLA Modules:
  0.0 109.2 jit_solution(11872748981721787207)
XLA Ops:
  0.6 102.4 %chain.1 = (bf16[128,4096]{1,0:T(8,128)(2,1)}, bf16[128,512]{1,0:T(8,128)(2,1)}, f32[8,128]{1,0:T(8,128)}, bf16[128,2048]{1,0:T(8,128)(2,1)}) custom-call(f32[8,128]{1,0:T(8,128)} %logits.1, s32[8]{0:T(128)} %ids_in.1, bf16[128,64,512]{2,1,0:T(8,128)(2,1)} %sp_hbm.1, bf16[4096,512]{1,0:T(8,128)(2,1)} %kw_hbm.1, bf16[4096,512]{1,0:T(8,128)(2,1)} %vw_hbm.1, ...), custom_call_target="tpu_custom_call" | custom-call | tf_op jit(solution)/shard_map/chain/pallas_call | solution.py:461
  103.1 0.0 copy-start
  103.1 0.0 copy-start.1
  103.1 4.6 %source_grad.1 = f32[128,16,512]{2,1,0:T(8,128)} custom-call(bf16[128,2048]{1,0:T(8,128)(2,1)} %get-tuple-element.8.w_ref, bf16[128,512]{1,0:T(8,128)(2,1)} %get-tuple-element.9.tile_ref), custom_call_target="tpu_custom_call" | custom-call | tf_op jit(solution)/shard_map/source_grad/pallas_call | solution.py:509
  107.7 0.0 copy-done
  107.7 1.0 copy.14
  108.6 0.0 copy-done.1
  108.6 0.6 copy.15
Async XLA Ops:
  103.1 4.6 %copy-start = (bf16[128,4096]{1,0:T(8,128)(2,1)S(1)}, bf16[128,4096]{1,0:T(8,128)(2,1)}, u32[]{:S(2)}) copy-start(bf16[128,4096]{1,0:T(8,128)(2,1)} %get-tuple-element.7) | copy-start | bytes 3145732
  103.1 5.5 %copy-start.1 = (f32[8,128]{1,0:T(8,128)S(1)}, f32[8,128]{1,0:T(8,128)}, u32[]{:S(2)}) copy-start(f32[8,128]{1,0:T(8,128)} %get-tuple-element.16) | copy-start | bytes 12292

commit v3 on v2

--- a/solution.py
+++ b/solution.py
@@ -157,8 +157,8 @@
 def chain_kernel(
     ndp, nmp,
     logits, ids_in, sp_hbm, kw_hbm, vw_hbm, q_hbm, k_hbm, v_hbm, c_hbm,
-    att_out, tile_out, lg_out, w_out,
-    p_v, kw_v, vw_v, q_v, k_v, v_v, c_v,
+    att_hbm, tile_out, lg_out, w_hbm,
+    att_out, w_out, p_v, kw_v, vw_v, q_v, k_v, v_v, c_v,
     mixed, ids_own, ids_buf, sbuf, pair, gr, rbuf, ys, yr, zs, zr, wp, wbuf,
     lsem, gs, gv, fs, fv, js, jv, bs, bv, cs, cv, us, uv, ts, tv, ws, wv,
 ):
@@ -236,6 +236,8 @@
     loads[0].wait()
     for c in loads[1:]:
         c.start()
+    w_save = pltpu.make_async_copy(w_out, w_hbm, lsem.at[9])
+    w_save.start()
     mixed[m] = mm(w_out[...], p_v[...].reshape(spn, width)).astype(BF)
 
     pl.semaphore_wait(barrier, n - 1)
@@ -372,6 +374,8 @@
             c_copy(g * ndp + dd).start()
 
     own_c.wait()
+    att_save = pltpu.make_async_copy(att_out, att_hbm, lsem.at[10])
+    att_save.start()
 
     @pl.loop(1, n)
     def _(k):
@@ -422,6 +426,8 @@
     def _(k):
         w_copy(k).start()
 
+    w_save.wait()
+    att_save.wait()
     for c in gat + fwd + yc + zc[1:]:
         c.wait_send()
 
@@ -438,7 +444,9 @@
     lg_out[...] = mix * (wg - jnp.sum(mix * wg, axis=1, keepdims=True))
 
 
-def source_kernel(w_ref, tile_ref, out_ref):
+def source_kernel(w_ref, tile_ref, att_ref, lg_ref, out_ref, att_out, lg_out):
+    att_out[...] = att_ref[...]
+    lg_out[...] = lg_ref[...]
     got = mm(w_ref[...], tile_ref[...], 0, 0)
     out_ref[...] = got.reshape(out_ref.shape)
 
@@ -467,8 +475,10 @@
             jax.ShapeDtypeStruct((tp, spn), BF),
         ),
         in_specs=[vmem, pl.BlockSpec(memory_space=pltpu.SMEM)] + [hbm] * 7,
-        out_specs=(vmem,) * 4,
+        out_specs=(hbm, vmem, vmem, hbm),
         scratch_shapes=[
+            pltpu.VMEM((seq, full), BF),
+            pltpu.VMEM((tp, spn), BF),
             pltpu.VMEM((nsrc, rows, width), BF),
             pltpu.VMEM((full, width), BF),
             pltpu.VMEM((full, width), BF),
@@ -489,7 +499,7 @@
             pltpu.VMEM((nz, tp, width), BF),
             pltpu.VMEM((ntask, nsrc), F32),
             pltpu.VMEM((n, ntask, nsrc), F32),
-            dma((9,)),
+            dma((11,)),
             dma((nz,)), dma((nz,)), dma((nz,)), dma((nz,)),
             dma((ndp,)), dma((ndp,)),
             dma((n,)), dma((n,)), dma((n,)), dma((n,)),
@@ -505,18 +515,28 @@
         queries.reshape(seq, full), keys.reshape(seq, full),
         values.reshape(seq, full), cotangent.reshape(seq, full),
     )
-    steps = 4
-    source_grad = pl.pallas_call(
+    steps = 2
+    source_grad, attended, logits_grad = pl.pallas_call(
         source_kernel,
         grid=(steps,),
-        out_shape=jax.ShapeDtypeStruct((nsrc, rows, width), F32),
+        out_shape=(
+            jax.ShapeDtypeStruct((nsrc, rows, width), F32),
+            jax.ShapeDtypeStruct((seq, full), BF),
+            jax.ShapeDtypeStruct((ntask, nsrc), F32),
+        ),
         in_specs=[
             pl.BlockSpec((tp, spn // steps), lambda i: (0, i)),
             pl.BlockSpec((tp, width), lambda i: (0, 0)),
+            pl.BlockSpec((seq // steps, full), lambda i: (i, 0)),
+            pl.BlockSpec((ntask, nsrc), lambda i: (0, 0)),
         ],
-        out_specs=pl.BlockSpec((nsrc // steps, rows, width), lambda i: (i, 0, 0)),
+        out_specs=(
+            pl.BlockSpec((nsrc // steps, rows, width), lambda i: (i, 0, 0)),
+            pl.BlockSpec((seq // steps, full), lambda i: (i, 0)),
+            pl.BlockSpec((ntask, nsrc), lambda i: (0, 0)),
+        ),
         name="source_grad",
-    )(w_big, tile)
+    )(w_big, tile, attended, logits_grad)
     return (attended.reshape(queries.shape), source_grad, logits_grad)
 
 

time: 109 us -> 107 us (0.982)
  local copies, waits for them, and re-layouts: 1.57 us -> 0 us
    unnamed x6 -> x0, local copies, waits for them, and re-layouts: 1.57 us -> none
where the time goes in v3:
time: 107 us
  Pallas kernels  106 us (99%)
    pallas_call x1, Pallas kernels, per_device(): pl.pallas_call(functools.partial(chain_kernel, ndp, nmp), out_shape=(jax....  102 us
    pallas_call x1, Pallas kernels, per_device(): pl.pallas_call(source_kernel, grid=(steps,), out_shape=(jax.ShapeDtypeStr...  3.95 us

profile of v3, /device:TPU:0, one launch (start us, length us, event | category | flops | bytes accessed | tf_op | source)
XLA Modules:
  0.0 106.5 jit_solution(6707114362149167255)
XLA Ops:
  0.6 101.9 %chain.1 = (bf16[128,4096]{1,0:T(8,128)(2,1)}, bf16[128,512]{1,0:T(8,128)(2,1)}, f32[8,128]{1,0:T(8,128)}, bf16[128,2048]{1,0:T(8,128)(2,1)}) custom-call(f32[8,128]{1,0:T(8,128)} %logits.1, s32[8]{0:T(128)} %ids_in.1, bf16[128,64,512]{2,1,0:T(8,128)(2,1)} %sp_hbm.1, bf16[4096,512]{1,0:T(8,128)(2,1)} %kw_hbm.1, bf16[4096,512]{1,0:T(8,128)(2,1)} %vw_hbm.1, ...), custom_call_target="tpu_custom_call" | custom-call | tf_op jit(solution)/shard_map/chain/pallas_call | solution.py:469
  102.6 3.9 %source_grad.1 = (f32[128,16,512]{2,1,0:T(8,128)}, bf16[128,4096]{1,0:T(8,128)(2,1)}, f32[8,128]{1,0:T(8,128)}) custom-call(bf16[128,2048]{1,0:T(8,128)(2,1)} %get-tuple-element.10.w_ref, bf16[128,512]{1,0:T(8,128)(2,1)} %get-tuple-element.11.tile_ref, bf16[128,4096]{1,0:T(8,128)(2,1)} %get-tuple-element.12.att_ref, f32[8,128]{1,0:T(8,128)} %get-tuple-element.13.lg_ref), custom_call_target="tpu_custom_call" | custom-call | tf_op jit(solution)/shard_map/source_grad/pallas_call | solution.py:519

commit v4 on v3

--- a/solution.py
+++ b/solution.py
@@ -305,9 +305,18 @@
     own_b = pltpu.make_async_copy(sbuf.at[me], pair.at[:, my_rows, my_cols], lsem.at[7])
     own_b.start()
 
-    @pl.loop(1, n)
-    def _(k):
-        b_copy(k).start()
+    def turn(t):
+        return lax.rem(t + nmp // 2 - 1 + t // (nmp // 2 + 1), nmp)
+
+    @pl.loop(1, nmp)
+    def _(t):
+        @pl.loop(0, ndp)
+        def _(dd):
+            b_copy(turn(t) * ndp + dd).start()
+
+    @pl.loop(1, ndp)
+    def _(dd):
+        b_copy(dd).start()
 
     for c in loads[3:]:
         c.wait()
@@ -366,7 +375,8 @@
         c_copy(dd).start()
 
     @pl.loop(1, nmp)
-    def _(g):
+    def _(t):
+        g = turn(t)
         group(g, 0)
 
         @pl.loop(0, ndp)
@@ -458,7 +468,7 @@
     ntask = task_logits.shape[0]
     ge = task_ids.shape[0]
     rows = ptok // ndp
-    if width % DH or nmp % 2 or ge != nmp or ptok % ndp or rows % 16 or rows & (rows - 1) or ntask * rows != 128:
+    if width % DH or nmp % 4 or ge != nmp or ptok % ndp or rows % 16 or rows & (rows - 1) or ntask * rows != 128:
         return on_device(*args)
     n, nz = ndp * nmp, nmp // 2
     tp, spn = ntask * rows, nsrc * rows

time: 107 us -> 106 us (level)
  no operation moved by 1% of the time
where the time goes in v4:
time: 106 us
  Pallas kernels  105 us (99%)
    pallas_call x1, Pallas kernels, per_device(): pl.pallas_call(functools.partial(chain_kernel, ndp, nmp), out_shape=(jax....  101 us
    pallas_call x1, Pallas kernels, per_device(): pl.pallas_call(source_kernel, grid=(steps,), out_shape=(jax.ShapeDtypeStr...  3.95 us

profile of v4, /device:TPU:0, one launch (start us, length us, event | category | flops | bytes accessed | tf_op | source)
XLA Modules:
  0.0 105.5 jit_solution(6064105265034195135)
XLA Ops:
  0.6 100.9 %chain.1 = (bf16[128,4096]{1,0:T(8,128)(2,1)}, bf16[128,512]{1,0:T(8,128)(2,1)}, f32[8,128]{1,0:T(8,128)}, bf16[128,2048]{1,0:T(8,128)(2,1)}) custom-call(f32[8,128]{1,0:T(8,128)} %logits.1, s32[8]{0:T(128)} %ids_in.1, bf16[128,64,512]{2,1,0:T(8,128)(2,1)} %sp_hbm.1, bf16[4096,512]{1,0:T(8,128)(2,1)} %kw_hbm.1, bf16[4096,512]{1,0:T(8,128)(2,1)} %vw_hbm.1, ...), custom_call_target="tpu_custom_call" | custom-call | tf_op jit(solution)/shard_map/chain/pallas_call | solution.py:479
  101.6 4.0 %source_grad.1 = (f32[128,16,512]{2,1,0:T(8,128)}, bf16[128,4096]{1,0:T(8,128)(2,1)}, f32[8,128]{1,0:T(8,128)}) custom-call(bf16[128,2048]{1,0:T(8,128)(2,1)} %get-tuple-element.10.w_ref, bf16[128,512]{1,0:T(8,128)(2,1)} %get-tuple-element.11.tile_ref, bf16[128,4096]{1,0:T(8,128)(2,1)} %get-tuple-element.12.att_ref, f32[8,128]{1,0:T(8,128)} %get-tuple-element.13.lg_ref), custom_call_target="tpu_custom_call" | custom-call | tf_op jit(solution)/shard_map/source_grad/pallas_call | solution.py:529
